TPU v7x, 32 devices: a whole 2x2x4 slice. The times are simulated.
32 devices in a mesh: parts: 2 (over x), rows: 16 (over z, y, core).
Axes of the slice: x: 2, y: 2, z: 4, core: 2. Of those that a mesh axis runs over, the one named last changes fastest.
Arguments:
- rhs: float32 [3, 12288, 256], P(None, 'rows', 'parts'), parts along dimension 2, may hold values from -6 to 6
- diag_inv: float32 [3, 12288, 768], P(None, 'rows'), may hold values from -0.21875 to 0.21875
- tiles: float32 [2, 32, 768, 768], P(None, 'rows'), may hold values from -0.15625 to 0.15625
- dest: int32 [2, 16, 2], P(None, 'rows'), may hold values from 0 to 15, all different within a row; in each aligned block of 16 rows (0 to 15, 16 to 31, ..., all dimensions but the last counted through in order) at most 4 rows name the same one
- obs_weight: float32 [12288], P('rows'), may hold values from -0.108253175 to 0.108253175, as said below
Outputs:
- solution: float32 [3, 12288, 256], P(None, 'rows', 'parts'), parts along dimension 2
- observed: float32 [256], P('parts'), parts along dimension 0
There are 2 independent parts, one for each index of `parts`. A program takes and returns all parts, laid end to end along the dimension named above; an argument that names none is the same for every part. Nothing has to cross between parts.
Inputs may be any that keep to these rules, and one draw needn't show every extreme that they name: `dest`: in each of the two levels, the two entries of a supernode differ, and no supernode of the next level is named more than 4 times. `obs_weight`: finite weights.
All inputs are finite; a program needn't handle non-finite values.
Results may differ from a plain program's by a relative error of at most 0.00029.
Values sent between devices are 32-bit elements; how exact they have to be, the bound alone decides.
No kernel may reach another device: no remote copies, remote signals or barrier semaphores. Data moves between devices by JAX's collectives and lax.ppermute only.
A program may use at most 128 MiB of HBM per device.

v0:
```python
import jax
import jax.numpy as jnp
from jax import lax
from jax.sharding import PartitionSpec as P


def collect_updates(solved_block, tiles_level, pattern_level):
    products = jnp.einsum(
        "kab,bc->kac",
        tiles_level,
        solved_block,
        precision=lax.Precision.HIGHEST,
        preferred_element_type=jnp.float32,
    )
    block_rows = solved_block.shape[0]
    width = products.shape[2]
    count = lax.axis_size("rows")
    sliced = lax.all_to_all(products, "rows", split_axis=1, concat_axis=0, tiled=True)
    owners = jnp.arange(count, dtype=jnp.int32)
    flat_targets = pattern_level.reshape(-1)
    matches = (owners[:, None] == flat_targets[None, :]).astype(jnp.float32)
    partial_value = jnp.einsum("mq,qac->mac", matches, sliced, precision=lax.Precision.HIGHEST)
    returned = lax.all_to_all(partial_value, "rows", split_axis=0, concat_axis=0, tiled=True)
    return returned.reshape(block_rows, width)


def body(rhs, diag_inv, tiles, dest, obs_weight):
    pattern = lax.all_gather(dest, "rows", axis=1, tiled=True)
    current = rhs[0]
    solved_levels = []
    solved_block = current
    for section in range(3):
        solved_block = jnp.dot(
            diag_inv[section],
            current,
            precision=lax.Precision.HIGHEST,
            preferred_element_type=jnp.float32,
        )
        solved_levels.append(solved_block)
        if section < 2:
            current = rhs[section + 1] - collect_updates(
                solved_block, tiles[section], pattern[section]
            )
    partial_sum = jnp.dot(
        obs_weight,
        solved_block,
        precision=lax.Precision.HIGHEST,
        preferred_element_type=jnp.float32,
    )
    observed = lax.psum(partial_sum, "rows")
    return (jnp.stack(solved_levels), observed)


def solution(mesh):
    in_specs = (
        P(None, "rows", "parts"),
        P(None, "rows", None),
        P(None, "rows", None, None),
        P(None, "rows", None),
        P("rows"),
    )
    out_specs = (P(None, "rows", "parts"), P("parts"))
    return jax.shard_map(body, mesh=mesh, in_specs=in_specs, out_specs=out_specs, check_vma=False)
```

profile of v0, /device:TPU:0, one launch (start us, length us, event | category | flops | bytes accessed | tf_op | source)
XLA Modules:
  0.0 156.5 jit_solution(14306570408259959369)
XLA Ops:
  0.6 3.7 %fusion.10 = f32[768,128]{1,0:T(8,128)S(1)} fusion(f32[3,768,768]{2,1,0:T(8,128)} %param.6, f32[3,768,128]{2,1,0:T(8,128)} %param.5), kind=kOutput, calls=%fused_computation.10 | convolution fusion | flops 905969664 | bytes 3145728 | tf_op jit(solution)/shard_map/dot_general | solution.py:33
  4.3 7.4 %fusion.15 = f32[2,768,128]{1,2,0:T(8,128)S(1)} fusion(f32[2,2,768,768]{3,2,1,0:T(8,128)} %param.7, f32[768,128]{1,0:T(8,128)S(1)} %fusion.10), kind=kOutput, calls=%fused_computation.15 | convolution fusion | flops 1811939328 | bytes 5898240 | tf_op jit(solution)/shard_map/kab,bc->kac/dot_general | solution.py:8
  11.7 1.2 copy.23
  12.9 7.5 %all-to-all-start = ((f32[2,768,128]{2,0,1:T(2,128)}), f32[2,768,128]{2,0,1:T(2,128)S(1)}, u32[]{:S(2)}, u32[]{:S(2)}) async-start(f32[2,768,128]{2,0,1:T(2,128)} %copy.23), calls=%async_computation | async-start | bytes 1572864 | tf_op jit(solution)/shard_map/all_to_all | solution.py:18
  20.4 29.2 %all_gather.3 = s32[2,16,2]{2,0,1:T(2,128)S(1)} all-gather(s32[2,1,2]{2,0,1:T(2,128)S(1)} %bitcast.82), channel_id=1, replica_groups=mesh['parts'=2,'rows'=16] {'rows'}, dimensions={1}, use_global_device_ids=true | all-gather | bytes 272 | tf_op jit(solution)/shard_map/all_gather | solution.py:28
  49.8 0.6 copy.25
  50.5 0.4 fusion.29
  50.8 0.1 copy.26
  51.0 16.7 %all_to_all.46 = f32[16,48,128]{2,1,0:T(8,128)S(1)} all-to-all(f32[16,48,128]{2,1,0:T(8,128)S(1)} %copy.26), channel_id=1, replica_groups=mesh['parts'=2,'rows'=16] {'rows'}, dimensions={0} | all-to-all | bytes 786432 | tf_op jit(solution)/shard_map/all_to_all | solution.py:23
  67.8 3.8 %fusion.8 = f32[128,768]{1,0:T(8,128)S(1)} fusion(f32[3,768,768]{2,1,0:T(8,128)} %param.6, f32[1,768,128]{2,1,0:T(8,128)S(1)} %bitcast_subtract_fusion.1), kind=kOutput, calls=%fused_computation.8 | convolution fusion | flops 905969664 | bytes 3145728 | tf_op jit(solution)/shard_map/dot_general | solution.py:33
  71.5 5.0 %fusion.18 = f32[2,768,128]{1,2,0:T(8,128)S(1)} fusion(f32[2,2,768,768]{3,2,1,0:T(8,128)S(1)} %copy-done, f32[128,768]{1,0:T(8,128)S(1)} %fusion.8), kind=kOutput, calls=%fused_computation.16 | convolution fusion | flops 1811939328 | bytes 5898240 | tf_op jit(solution)/shard_map/kab,bc->kac/dot_general | solution.py:8
  76.5 1.2 copy.28
  77.7 3.6 %all-to-all-start.2 = ((f32[2,768,128]{2,0,1:T(2,128)}), f32[2,768,128]{2,0,1:T(2,128)S(1)}, u32[]{:S(2)}, u32[]{:S(2)}) async-start(f32[2,768,128]{2,0,1:T(2,128)} %copy.28), calls=%async_computation.2 | async-start | bytes 1572864 | tf_op jit(solution)/shard_map/all_to_all | solution.py:18
  81.4 18.6 %all-to-all-done.2 = f32[2,768,128]{2,0,1:T(2,128)S(1)} async-done(((f32[2,768,128]{2,0,1:T(2,128)}), f32[2,768,128]{2,0,1:T(2,128)S(1)}, u32[]{:S(2)}, u32[]{:S(2)}) %all-to-all-start.2) | async-done | bytes 786464 | tf_op jit(solution)/shard_map/all_to_all | solution.py:18
  100.0 0.6 copy.30
  100.6 0.4 fusion.32
  101.0 0.9 copy.31
  101.9 5.3 %all-to-all-start.3 = ((f32[16,48,128]{2,1,0:T(8,128)}), f32[16,48,128]{2,1,0:T(8,128)S(1)}, u32[]{:S(2)}, u32[]{:S(2)}) async-start(f32[16,48,128]{2,1,0:T(8,128)} %copy.31), calls=%async_computation.3 | async-start | bytes 786432 | tf_op jit(solution)/shard_map/all_to_all | solution.py:23
  107.3 0.2 copy.27
  107.4 12.0 %all-to-all-done.3 = f32[16,48,128]{2,1,0:T(8,128)S(1)} async-done(((f32[16,48,128]{2,1,0:T(8,128)}), f32[16,48,128]{2,1,0:T(8,128)S(1)}, u32[]{:S(2)}, u32[]{:S(2)}) %all-to-all-start.3) | async-done | bytes 393248 | tf_op jit(solution)/shard_map/all_to_all | solution.py:23
  119.4 3.7 %fusion.6 = f32[128,768]{0,1:T(8,128)S(1)} fusion(f32[3,768,768]{2,1,0:T(8,128)} %param.6, f32[1,768,128]{2,1,0:T(8,128)S(1)} %bitcast_subtract_fusion), kind=kOutput, calls=%fused_computation.6 | convolution fusion | flops 905969664 | bytes 3145728 | tf_op jit(solution)/shard_map/dot_general | solution.py:33
  123.1 0.3 convolution_bitcast_fusion
  123.4 32.0 %psum.7 = f32[128]{0:T(128)} all-reduce(f32[128]{0:T(128)S(1)} %convolution_bitcast_fusion), channel_id=1, replica_groups=mesh['parts'=2,'rows'=16] {'rows'}, use_global_device_ids=true, to_apply=%region_0.0 | all-reduce | flops 128 | bytes 1024 | tf_op jit(solution)/shard_map/psum | solution.py:50
  155.4 1.1 pad_maximum_fusion
  (17 shorter events, 0.4 us)
Async XLA Ops:
  11.7 8.7 %copy-start.3 = (s32[2,1,2]{2,1,0:T(1,128)S(1)}, s32[2,1,2]{2,1,0:T(1,128)}, u32[]{:S(2)}) copy-start(s32[2,1,2]{2,1,0:T(1,128)} %param.8) | copy-start | bytes 52
  12.9 54.8 %copy-start.1 = (f32[3,768,128]{2,1,0:T(8,128)S(1)}, f32[3,768,128]{2,1,0:T(8,128)}, u32[]{:S(2)}) copy-start(f32[3,768,128]{2,1,0:T(8,128)} %param.5) | copy-start | bytes 3538948
  12.9 36.9 %all-to-all-start = ((f32[2,768,128]{2,0,1:T(2,128)}), f32[2,768,128]{2,0,1:T(2,128)S(1)}, u32[]{:S(2)}, u32[]{:S(2)}) async-start(f32[2,768,128]{2,0,1:T(2,128)} %copy.23), calls=%async_computation | async-start | bytes 1572864 | tf_op jit(solution)/shard_map/all_to_all | solution.py:18
  49.8 21.8 %copy-start = (f32[2,2,768,768]{3,2,1,0:T(8,128)S(1)}, f32[2,2,768,768]{3,2,1,0:T(8,128)}, u32[]{:S(2)}) copy-start(f32[2,2,768,768]{3,2,1,0:T(8,128)} %param.7) | copy-start | bytes 28311556
  77.7 22.3 %all-to-all-start.2 = ((f32[2,768,128]{2,0,1:T(2,128)}), f32[2,768,128]{2,0,1:T(2,128)S(1)}, u32[]{:S(2)}, u32[]{:S(2)}) async-start(f32[2,768,128]{2,0,1:T(2,128)} %copy.28), calls=%async_computation.2 | async-start | bytes 1572864 | tf_op jit(solution)/shard_map/all_to_all | solution.py:18
  100.0 7.2 %copy-start.2 = (f32[768]{0:T(1024)S(1)}, f32[768]{0:T(1024)}, u32[]{:S(2)}) copy-start(f32[768]{0:T(1024)} %param.9) | copy-start | bytes 9220
  101.9 17.5 %all-to-all-start.3 = ((f32[16,48,128]{2,1,0:T(8,128)}), f32[16,48,128]{2,1,0:T(8,128)S(1)}, u32[]{:S(2)}, u32[]{:S(2)}) async-start(f32[16,48,128]{2,1,0:T(8,128)} %copy.31), calls=%async_computation.3 | async-start | bytes 786432 | tf_op jit(solution)/shard_map/all_to_all | solution.py:23
where the time goes:
time: 157 us
  blocking collectives  77.9 us (50%)
  waiting for transfers between devices  30.5 us (19%)
  matrix products  24.5 us (16%)
  starting transfers between devices  16.5 us (11%)
  local copies, waits for them, and re-layouts  5.05 us (3%)
    psum x1, blocking collectives, body(): observed = lax.psum(partial_sum, 'rows')  32 us
    all_gather x1, blocking collectives, body(): pattern = lax.all_gather(dest, 'rows', axis=1, tiled=True)  29.2 us
    all_to_all x2, waiting for transfers between devices, collect_updates(): lax.all_to_all(products, 'rows', split_axis=1, concat_axis=0, tiled=True)  18.6 us
    all_to_all x1, blocking collectives, collect_updates(): lax.all_to_all(partial_value, 'rows', split_axis=0, concat_axis=0, tiled=...  16.7 us
    dot_general x2, matrix products, collect_updates(): jnp.einsum('kab,bc->kac', tiles_level, solved_block, precision=lax.Precis...  12.3 us
    all_to_all x1, waiting for transfers between devices, collect_updates(): lax.all_to_all(partial_value, 'rows', split_axis=0, concat_axis=0, tiled=...  12 us
    all_to_all x2, starting transfers between devices, collect_updates(): lax.all_to_all(products, 'rows', split_axis=1, concat_axis=0, tiled=True)  11.2 us
    dot_general x3, matrix products, body(): jnp.dot(diag_inv[section], current, precision=lax.Precision.HIGHEST, pref...  11.1 us
  transfers between devices with their start and end apart: 3, of which 2 were waited for; matrix products, arithmetic and copies ran while one was open for 0% of the time, Pallas kernels for 0%

commit v1 on v0

--- a/solution.py
+++ b/solution.py
@@ -2,6 +2,15 @@
 import jax.numpy as jnp
 from jax import lax
 from jax.sharding import PartitionSpec as P
+
+
+def added_up(x, mesh_axis):
+    size = lax.axis_size(mesh_axis)
+    total, stride = (x, 1)
+    while stride < size:
+        total = total + lax.ppermute(total, mesh_axis, [(i, i ^ stride) for i in range(size)])
+        stride = 2 * stride
+    return total
 
 
 def collect_updates(solved_block, tiles_level, pattern_level):
@@ -47,7 +56,7 @@
         precision=lax.Precision.HIGHEST,
         preferred_element_type=jnp.float32,
     )
-    observed = lax.psum(partial_sum, "rows")
+    observed = added_up(partial_sum, "rows")
     return (jnp.stack(solved_levels), observed)
 
 

time: 157 us -> 137 us (0.87)
  blocking collectives: 77.9 us -> 45.9 us
  waiting for transfers between devices: 30.5 us -> 38.8 us
  starting transfers between devices: 16.5 us -> 20 us
    psum x1 -> x0, blocking collectives: 32 us -> none  [body(): observed = lax.psum(partial_sum, 'rows')]
    ppermute x0 -> x4, waiting for transfers between devices: none -> 8.08 us  [added_up(): lax.ppermute(total, mesh_axis, [(i, i ^ stride) for i in range(size)])]
    ppermute x0 -> x4, starting transfers between devices: none -> 3.49 us  [added_up(): lax.ppermute(total, mesh_axis, [(i, i ^ stride) for i in range(size)])]
  transfers between devices with their start and end apart: 3 -> 7, of which waited for: 2 -> 6; matrix products, arithmetic and copies ran while one was open for 0% -> 1% of each run, Pallas kernels for 0% -> 0%
where the time goes in v1:
time: 137 us
  blocking collectives  45.9 us (34%)
  waiting for transfers between devices  38.8 us (28%)
  matrix products  24.5 us (18%)
  starting transfers between devices  20 us (15%)
  local copies, waits for them, and re-layouts  5.05 us (4%)
  other arithmetic  1.71 us (1%)
    all_gather x1, blocking collectives, body(): pattern = lax.all_gather(dest, 'rows', axis=1, tiled=True)  29.2 us
    all_to_all x2, waiting for transfers between devices, collect_updates(): lax.all_to_all(products, 'rows', split_axis=1, concat_axis=0, tiled=True)  18.6 us
    all_to_all x1, blocking collectives, collect_updates(): lax.all_to_all(partial_value, 'rows', split_axis=0, concat_axis=0, tiled=...  16.7 us
    dot_general x2, matrix products, collect_updates(): jnp.einsum('kab,bc->kac', tiles_level, solved_block, precision=lax.Precis...  12.3 us
    all_to_all x1, waiting for transfers between devices, collect_updates(): lax.all_to_all(partial_value, 'rows', split_axis=0, concat_axis=0, tiled=...  12.1 us
    all_to_all x2, starting transfers between devices, collect_updates(): lax.all_to_all(products, 'rows', split_axis=1, concat_axis=0, tiled=True)  11.2 us
    dot_general x3, matrix products, body(): jnp.dot(diag_inv[section], current, precision=lax.Precision.HIGHEST, pref...  11.1 us
    ppermute x4, waiting for transfers between devices, added_up(): lax.ppermute(total, mesh_axis, [(i, i ^ stride) for i in range(size)])  8.08 us
  transfers between devices with their start and end apart: 7, of which 6 were waited for; matrix products, arithmetic and copies ran while one was open for 1% of the time, Pallas kernels for 0%

profile of v1, /device:TPU:0, one launch (start us, length us, event | category | flops | bytes accessed | tf_op | source)
XLA Modules:
  0.0 136.8 jit_solution(7946217344844319423)
XLA Ops:
  0.6 3.7 %fusion.10 = f32[768,128]{1,0:T(8,128)S(1)} fusion(f32[3,768,768]{2,1,0:T(8,128)} %param.6, f32[3,768,128]{2,1,0:T(8,128)} %param.5), kind=kOutput, calls=%fused_computation.10 | convolution fusion | flops 905969664 | bytes 3145728 | tf_op jit(solution)/shard_map/dot_general | solution.py:42
  4.3 7.4 %fusion.15 = f32[2,768,128]{1,2,0:T(8,128)S(1)} fusion(f32[2,2,768,768]{3,2,1,0:T(8,128)} %param.7, f32[768,128]{1,0:T(8,128)S(1)} %fusion.10), kind=kOutput, calls=%fused_computation.15 | convolution fusion | flops 1811939328 | bytes 5898240 | tf_op jit(solution)/shard_map/kab,bc->kac/dot_general | solution.py:17
  11.7 1.2 copy.23
  12.9 7.5 %all-to-all-start = ((f32[2,768,128]{2,0,1:T(2,128)}), f32[2,768,128]{2,0,1:T(2,128)S(1)}, u32[]{:S(2)}, u32[]{:S(2)}) async-start(f32[2,768,128]{2,0,1:T(2,128)} %copy.23), calls=%async_computation | async-start | bytes 1572864 | tf_op jit(solution)/shard_map/all_to_all | solution.py:27
  20.4 29.2 %all_gather.3 = s32[2,16,2]{2,0,1:T(2,128)S(1)} all-gather(s32[2,1,2]{2,0,1:T(2,128)S(1)} %bitcast.82), channel_id=1, replica_groups=mesh['parts'=2,'rows'=16] {'rows'}, dimensions={1}, use_global_device_ids=true | all-gather | bytes 272 | tf_op jit(solution)/shard_map/all_gather | solution.py:37
  49.8 0.6 copy.25
  51.0 16.7 %all_to_all.46 = f32[16,48,128]{2,1,0:T(8,128)S(1)} all-to-all(f32[16,48,128]{2,1,0:T(8,128)S(1)} %copy.26), channel_id=1, replica_groups=mesh['parts'=2,'rows'=16] {'rows'}, dimensions={0} | all-to-all | bytes 786432 | tf_op jit(solution)/shard_map/all_to_all | solution.py:32
  67.8 3.8 %fusion.8 = f32[128,768]{1,0:T(8,128)S(1)} fusion(f32[3,768,768]{2,1,0:T(8,128)} %param.6, f32[1,768,128]{2,1,0:T(8,128)S(1)} %bitcast_subtract_fusion.1), kind=kOutput, calls=%fused_computation.8 | convolution fusion | flops 905969664 | bytes 3145728 | tf_op jit(solution)/shard_map/dot_general | solution.py:42
  71.5 5.0 %fusion.18 = f32[2,768,128]{1,2,0:T(8,128)S(1)} fusion(f32[2,2,768,768]{3,2,1,0:T(8,128)S(1)} %copy-done, f32[128,768]{1,0:T(8,128)S(1)} %fusion.8), kind=kOutput, calls=%fused_computation.16 | convolution fusion | flops 1811939328 | bytes 5898240 | tf_op jit(solution)/shard_map/kab,bc->kac/dot_general | solution.py:17
  76.5 1.2 copy.28
  77.7 3.6 %all-to-all-start.2 = ((f32[2,768,128]{2,0,1:T(2,128)}), f32[2,768,128]{2,0,1:T(2,128)S(1)}, u32[]{:S(2)}, u32[]{:S(2)}) async-start(f32[2,768,128]{2,0,1:T(2,128)} %copy.28), calls=%async_computation.2 | async-start | bytes 1572864 | tf_op jit(solution)/shard_map/all_to_all | solution.py:27
  81.4 18.6 %all-to-all-done.2 = f32[2,768,128]{2,0,1:T(2,128)S(1)} async-done(((f32[2,768,128]{2,0,1:T(2,128)}), f32[2,768,128]{2,0,1:T(2,128)S(1)}, u32[]{:S(2)}, u32[]{:S(2)}) %all-to-all-start.2) | async-done | bytes 786464 | tf_op jit(solution)/shard_map/all_to_all | solution.py:27
  101.0 0.9 copy.31
  101.9 5.3 %all-to-all-start.3 = ((f32[16,48,128]{2,1,0:T(8,128)}), f32[16,48,128]{2,1,0:T(8,128)S(1)}, u32[]{:S(2)}, u32[]{:S(2)}) async-start(f32[16,48,128]{2,1,0:T(8,128)} %copy.31), calls=%async_computation.3 | async-start | bytes 786432 | tf_op jit(solution)/shard_map/all_to_all | solution.py:32
  107.3 12.1 %all-to-all-done.3 = f32[16,48,128]{2,1,0:T(8,128)S(1)} async-done(((f32[16,48,128]{2,1,0:T(8,128)}), f32[16,48,128]{2,1,0:T(8,128)S(1)}, u32[]{:S(2)}, u32[]{:S(2)}) %all-to-all-start.3) | async-done | bytes 393248 | tf_op jit(solution)/shard_map/all_to_all | solution.py:32
  119.4 3.7 %fusion.6 = f32[128,768]{0,1:T(8,128)S(1)} fusion(f32[3,768,768]{2,1,0:T(8,128)} %param.6, f32[1,768,128]{2,1,0:T(8,128)S(1)} %bitcast_subtract_fusion), kind=kOutput, calls=%fused_computation.6 | convolution fusion | flops 905969664 | bytes 3145728 | tf_op jit(solution)/shard_map/dot_general | solution.py:42
  123.6 1.0 collective-permute-done
  124.6 0.7 collective-permute-start.1
  125.3 2.9 %collective-permute-done.1 = f32[128]{0:T(128)S(1)} collective-permute-done((f32[128]{0:T(128)S(1)}, f32[128]{0:T(128)S(1)}, u32[]{:S(2)}, u32[]{:S(2)}) %collective-permute-start.1) | collective-permute-done | bytes 544 | tf_op jit(solution)/shard_map/ppermute | solution.py:11
  128.2 0.9 collective-permute-start.2
  129.3 2.5 %collective-permute-done.2 = f32[128]{0:T(128)S(1)} collective-permute-done((f32[128]{0:T(128)S(1)}, f32[128]{0:T(128)S(1)}, u32[]{:S(2)}, u32[]{:S(2)}) %collective-permute-start.2) | collective-permute-done | bytes 544 | tf_op jit(solution)/shard_map/ppermute | solution.py:11
  131.8 1.7 %collective-permute-start.3 = (f32[128]{0:T(128)S(1)}, f32[128]{0:T(128)S(1)}, u32[]{:S(2)}, u32[]{:S(2)}) collective-permute-start(f32[128]{0:T(128)S(1)} %add.14), channel_id=1, source_target_pairs={{0,8},{1,9},{2,10},{3,11},{4,12},{5,13},{6,14},{7,15},{8,0},{9,1},... | collective-permute-start | bytes 1544 | tf_op jit(solution)/shard_map/ppermute | solution.py:11
  133.5 1.1 pad_maximum_fusion
  134.6 1.7 %collective-permute-done.3 = f32[128]{0:T(128)S(1)} collective-permute-done((f32[128]{0:T(128)S(1)}, f32[128]{0:T(128)S(1)}, u32[]{:S(2)}, u32[]{:S(2)}) %collective-permute-start.3) | collective-permute-done | bytes 544 | tf_op jit(solution)/shard_map/ppermute | solution.py:11
  (28 shorter events, 3.1 us)
Async XLA Ops:
  11.7 8.7 %copy-start.3 = (s32[2,1,2]{2,1,0:T(1,128)S(1)}, s32[2,1,2]{2,1,0:T(1,128)}, u32[]{:S(2)}) copy-start(s32[2,1,2]{2,1,0:T(1,128)} %param.8) | copy-start | bytes 52
  12.9 54.8 %copy-start.1 = (f32[3,768,128]{2,1,0:T(8,128)S(1)}, f32[3,768,128]{2,1,0:T(8,128)}, u32[]{:S(2)}) copy-start(f32[3,768,128]{2,1,0:T(8,128)} %param.5) | copy-start | bytes 3538948
  12.9 36.9 %all-to-all-start = ((f32[2,768,128]{2,0,1:T(2,128)}), f32[2,768,128]{2,0,1:T(2,128)S(1)}, u32[]{:S(2)}, u32[]{:S(2)}) async-start(f32[2,768,128]{2,0,1:T(2,128)} %copy.23), calls=%async_computation | async-start | bytes 1572864 | tf_op jit(solution)/shard_map/all_to_all | solution.py:27
  49.8 21.8 %copy-start = (f32[2,2,768,768]{3,2,1,0:T(8,128)S(1)}, f32[2,2,768,768]{3,2,1,0:T(8,128)}, u32[]{:S(2)}) copy-start(f32[2,2,768,768]{3,2,1,0:T(8,128)} %param.7) | copy-start | bytes 28311556
  77.7 22.3 %all-to-all-start.2 = ((f32[2,768,128]{2,0,1:T(2,128)}), f32[2,768,128]{2,0,1:T(2,128)S(1)}, u32[]{:S(2)}, u32[]{:S(2)}) async-start(f32[2,768,128]{2,0,1:T(2,128)} %copy.28), calls=%async_computation.2 | async-start | bytes 1572864 | tf_op jit(solution)/shard_map/all_to_all | solution.py:27
  100.0 7.2 %copy-start.2 = (f32[768]{0:T(1024)S(1)}, f32[768]{0:T(1024)}, u32[]{:S(2)}) copy-start(f32[768]{0:T(1024)} %param.9) | copy-start | bytes 9220
  101.9 17.5 %all-to-all-start.3 = ((f32[16,48,128]{2,1,0:T(8,128)}), f32[16,48,128]{2,1,0:T(8,128)S(1)}, u32[]{:S(2)}, u32[]{:S(2)}) async-start(f32[16,48,128]{2,1,0:T(8,128)} %copy.31), calls=%async_computation.3 | async-start | bytes 786432 | tf_op jit(solution)/shard_map/all_to_all | solution.py:32
  123.4 1.2 collective-permute-start
  124.6 3.6 %collective-permute-start.1 = (f32[128]{0:T(128)S(1)}, f32[128]{0:T(128)S(1)}, u32[]{:S(2)}, u32[]{:S(2)}) collective-permute-start(f32[128]{0:T(128)S(1)} %add.12), channel_id=1, source_target_pairs={{0,2},{1,3},{2,0},{3,1},{4,6},{5,7},{6,4},{7,5},{8,10},{9,11},{10,... | collective-permute-start | bytes 1544 | tf_op jit(solution)/shard_map/ppermute | solution.py:11
  128.2 3.6 %collective-permute-start.2 = (f32[128]{0:T(128)S(1)}, f32[128]{0:T(128)S(1)}, u32[]{:S(2)}, u32[]{:S(2)}) collective-permute-start(f32[128]{0:T(128)S(1)} %add.13), channel_id=1, source_target_pairs={{0,4},{1,5},{2,6},{3,7},{4,0},{5,1},{6,2},{7,3},{8,12},{9,13},{10,... | collective-permute-start | bytes 1544 | tf_op jit(solution)/shard_map/ppermute | solution.py:11
  131.8 4.5 %collective-permute-start.3 = (f32[128]{0:T(128)S(1)}, f32[128]{0:T(128)S(1)}, u32[]{:S(2)}, u32[]{:S(2)}) collective-permute-start(f32[128]{0:T(128)S(1)} %add.14), channel_id=1, source_target_pairs={{0,8},{1,9},{2,10},{3,11},{4,12},{5,13},{6,14},{7,15},{8,0},{9,1},... | collective-permute-start | bytes 1544 | tf_op jit(solution)/shard_map/ppermute | solution.py:11
